TPU v7x, 256 devices: a whole 4x4x8 slice. The times are simulated.
256 devices in a mesh: section: 2 (over core), chan: 32 (over z, x), feed: 4 (over y).
Axes of the slice: x: 4, y: 4, z: 8, core: 2. Of those that a mesh axis runs over, the one named last changes fastest.
Arguments:
- voltages: bfloat16 [2, 1024, 24, 8192], P(None, 'feed', 'section', 'chan'), may hold values from -4 to 4
- positions: int32 [1024], replicated, may hold values from 0 to 1023, each once
- chan_delays: int32 [16, 8192], replicated, may hold values from 0 to 2
- sub_delays: int32 [256, 32], replicated, may hold values from 0 to 4
- boxcars: int32 [3, 2], replicated, may hold values from 1 to 6, as said below
Outputs:
- boxcar_snr: float32 [1024, 24, 3, 256], P(('chan', 'feed'), 'section')
Inputs may be any that keep to these rules, and one draw needn't show every extreme that they name: `boxcars`: column 0 holds the widths 2 to 4, each once; column 1 holds dilations of 1 or more with (width - 1) * dilation <= 6; the filter of width 2 has dilation 6 and the widest filter dilation 1.
All inputs are finite; a program needn't handle non-finite values.
Results may differ from a plain program's by a relative error of at most 0.0033.
Values may be sent and summed in bfloat16 or wider, within the bound.
A program may use at most 64 MiB of HBM per device.

v0:
```python
import math
import jax
import jax.numpy as jnp
from jax import lax
from jax.sharding import PartitionSpec as P

NF = 1024
C = 8192
NK = 16
ND = 256
NW = 3
D1MAX = 2
D2MAX = 4
BOXMAX = 6
SUBCH = 256
EPSILON = 1e-05


def beam_order(positions):
    chan = jnp.arange(32, dtype=jnp.int32)[None, :, None]
    feed = jnp.arange(4, dtype=jnp.int32)[:, None, None]
    low = jnp.arange(8, dtype=jnp.int32)[None, None, :]
    beam_ids = (chan * 32 + feed * 8 + low).reshape(NF)
    phase_ids = beam_ids[:, None] * positions[None, :] % NF
    angles = phase_ids.astype(jnp.float32) * (2.0 * math.pi / NF)
    cosine = jnp.cos(angles)
    sine = jnp.sin(angles)
    upper = jnp.concatenate([cosine, sine], axis=1)
    lower = jnp.concatenate([-sine, cosine], axis=1)
    return jnp.concatenate([upper, lower], axis=0).astype(jnp.bfloat16)


def two_part_dot(values, zero_one):
    high = values.astype(jnp.bfloat16)
    low = (values - high.astype(jnp.float32)).astype(jnp.bfloat16)
    first = jnp.dot(high, zero_one, preferred_element_type=jnp.float32)
    return first + jnp.dot(low, zero_one, preferred_element_type=jnp.float32)


def channel_selector(delays, span_t):
    local = delays.shape[1]
    times = jnp.arange(span_t, dtype=jnp.int32)[:, None, None, None]
    outs = jnp.arange(span_t + D1MAX, dtype=jnp.int32)[None, None, :, None]
    chosen = times + D1MAX - outs == jnp.transpose(delays)[None, :, None, :]
    return chosen.astype(jnp.bfloat16).reshape(span_t * local, (span_t + D1MAX) * NK)


def subband_selector(sub_delays):
    offsets = jnp.arange(D2MAX + 1, dtype=jnp.int32)[:, None, None, None]
    matches = jnp.transpose(sub_delays)[None, :, None, :] == offsets
    trial_k = jnp.arange(ND, dtype=jnp.int32) * NK // ND
    own = jnp.arange(NK, dtype=jnp.int32)[:, None] == trial_k[None, :]
    weights = matches & own[None, None, :, :]
    return weights.astype(jnp.bfloat16).reshape(D2MAX + 1, -1, ND)


def boxcar_filter(extended, boxcars, span_t):
    outputs = []
    for filter_index in range(NW):
        width_now = boxcars[filter_index, 0]
        stride_now = boxcars[filter_index, 1]
        summed = extended[:, :span_t]
        for offset in range(1, NW + 1):
            start = jnp.minimum(offset * stride_now, BOXMAX)
            window_part = lax.dynamic_slice_in_dim(extended, start, span_t, 1)
            summed = summed + jnp.where(offset < width_now, window_part, 0.0)
        outputs.append(summed * lax.rsqrt(width_now.astype(jnp.float32)))
    return jnp.stack(outputs, axis=2)


def per_device(voltages, positions, chan_delays, sub_delays, boxcars):
    gathered = lax.all_to_all(voltages, "feed", split_axis=3, concat_axis=1, tiled=True)
    span_t = gathered.shape[2]
    local = gathered.shape[3]
    table = beam_order(positions)
    flat = gathered.reshape(2 * NF, span_t * local)
    product = jnp.dot(table, flat, preferred_element_type=jnp.float32)
    real_part = product[:NF]
    imag_part = product[NF:]
    power = (real_part * real_part + imag_part * imag_part).reshape(NF, span_t, local)
    section_count = lax.axis_size("section")
    totals = lax.psum(jnp.sum(power, axis=1), "section")
    level = totals / (span_t * section_count)
    normed = power / (level[:, None, :] + EPSILON) - 1.0
    start = lax.axis_index("chan") * SUBCH + lax.axis_index("feed") * local
    delays = lax.dynamic_slice_in_dim(chan_delays, start, local, 1)
    partial = two_part_dot(normed.reshape(NF, span_t * local), channel_selector(delays, span_t))
    summed = lax.psum_scatter(partial, "feed", scatter_dimension=0, tiled=True)
    span_u = span_t + D1MAX
    blocks = summed.reshape(lax.axis_size("chan"), -1, span_u * NK)
    turned = lax.all_to_all(blocks, "chan", split_axis=0, concat_axis=0, tiled=True)
    bands, beams = (turned.shape[0], turned.shape[1])
    subband = jnp.transpose(turned.reshape(bands, beams, span_u, NK), (1, 2, 0, 3))
    padded = jnp.pad(subband.reshape(beams, span_u, bands * NK), ((0, 0), (D2MAX, D2MAX), (0, 0)))
    span_v = span_u + D2MAX
    shifted = jnp.concatenate([padded[:, d : d + span_v] for d in range(D2MAX + 1)], axis=2)
    weights = subband_selector(sub_delays).reshape(-1, ND)
    dedispersed = two_part_dot(shifted.reshape(beams * span_v, -1), weights) * (1.0 / math.sqrt(C))
    dedispersed = dedispersed.reshape(beams, span_v, ND)
    later = lax.ppermute(dedispersed[:, :span_t], "section", [(1, 0)])
    extended = jnp.pad(dedispersed[:, BOXMAX:], ((0, 0), (0, BOXMAX), (0, 0)))
    extended = extended + jnp.pad(later, ((0, 0), (BOXMAX, 0), (0, 0)))
    return boxcar_filter(extended, boxcars, span_t)


def solution(mesh):
    return jax.shard_map(
        per_device,
        mesh=mesh,
        in_specs=(P(None, "feed", "section", "chan"), P(), P(), P(), P()),
        out_specs=P(("chan", "feed"), "section", None, None),
        check_vma=False,
    )
```

profile of v0, /device:TPU:1, one launch (start us, length us, event | category | flops | bytes accessed | tf_op | source)
XLA Modules:
  0.0 219.8 jit_solution(1089772544984727857)
XLA Ops:
  6.5 8.9 %copy.44 = bf16[2,256,12,256]{1,0,2,3:T(2,128)(2,1)} copy(bf16[2,256,12,256]{3,1,2,0:T(8,128)(2,1)} %param.5) | data formatting | bytes 6291456 | tf_op args[0]
  15.4 5.1 %all-to-all-start = ((bf16[2,256,12,256]{1,0,2,3:T(2,128)(2,1)}), bf16[2,256,12,256]{1,0,2,3:T(2,128)(2,1)}, u32[]{:S(2)}, u32[]{:S(2)}) async-start(bf16[2,256,12,256]{1,0,2,3:T(2,128)(2,1)} %copy.44), calls=%async_computation | async-start | bytes 6291456 | tf_op jit(solution)/shard_map/all_to_all | solution.py:72
  20.6 0.1 iota_add_fusion
  20.7 0.1 add.154
  20.8 19.0 %fusion.14 = (bf16[1024,1024]{1,0:T(8,128)(2,1)S(1)}, bf16[1024,1024]{1,0:T(8,128)(2,1)}, bf16[1024,1024]{1,0:T(8,128)(2,1)}) fusion(s32[1024]{0:T(1024)S(1)} %copy-done.5, s32[1024]{0:T(1024)S(1)} %add.154), kind=kLoop, calls=%fused_computation.25 | loop fusion | flops 18874368 | bytes 6299648 | tf_op jit(solution)/shard_map/convert.5
  39.8 16.4 %all-to-all-done = bf16[2,256,12,256]{1,0,2,3:T(2,128)(2,1)} async-done(((bf16[2,256,12,256]{1,0,2,3:T(2,128)(2,1)}), bf16[2,256,12,256]{1,0,2,3:T(2,128)(2,1)}, u32[]{:S(2)}, u32[]{:S(2)}) %all-to-all-start) | async-done | bytes 3145760 | tf_op jit(solution)/shard_map/all_to_all | solution.py:72
  56.2 2.6 %copy.45 = bf16[2,256,12,256]{1,3,2,0:T(8,128)(2,1)S(1)} copy(bf16[2,256,12,256]{1,0,2,3:T(2,128)(2,1)} %all-to-all-done) | data formatting | bytes 6291456 | tf_op jit(solution)/shard_map/all_to_all | solution.py:72
  58.8 4.1 %copy.46 = bf16[2,4,256,12,64]{2,1,0,4,3:T(4,128)(2,1)} copy(bf16[2,4,256,12,64]{2,4,1,3,0:T(8,128)(2,1)S(1)} %bitcast.56) | data formatting | bytes 6291456 | tf_op jit(solution)/shard_map/all_to_all | solution.py:72
  62.9 6.1 %reshape.237 = bf16[2048,768]{0,1:T(8,128)(2,1)} reshape(bf16[2,4,256,12,64]{2,1,0,4,3:T(4,128)(2,1)} %copy.46) | data formatting | bytes 6291456 | tf_op jit(solution)/shard_map/reshape | solution.py:76
  69.0 16.8 %fusion = f32[2048,768]{0,1:T(8,128)S(1)} fusion(bf16[2048,768]{0,1:T(8,128)(2,1)} %reshape.237, bf16[1024,1024]{1,0:T(8,128)(2,1)} %get-tuple-element.16, bf16[1024,1024]{1,0:T(8,128)(2,1)} %get-tuple-element.15, bf16[1024,1024]{1,0:T(8,128)(2,1)S(1)} %get-tuple-element.14), kind=kOutput, calls=%fused_computation | convolution fusion | flops 6476005376 | bytes 15728640 | tf_op jit(solution)/shard_map/dot_general | solution.py:77
  85.9 2.8 %fusion.11 = f32[1024,768]{0,1:T(8,128)} fusion(f32[2048,768]{0,1:T(8,128)S(1)} %fusion), kind=kLoop, calls=%fused_computation.19 | loop fusion | flops 2359296 | bytes 9437184 | tf_op jit(solution)/shard_map/add | solution.py:80
  88.7 0.8 copy-done.1
  89.6 2.8 %reduce_sum.9 = f32[1024,64]{0,1:T(8,128)} reduce(f32[1024,12,64]{0,2,1:T(8,128)} %bitcast.57, f32[]{:T(128)} %constant.80.clone.1), dimensions={1}, to_apply=%region_0.1 | reduce | flops 720896 | bytes 3407876 | tf_op jit(solution)/shard_map/reduce_sum | solution.py:82
  92.4 0.2 reduce-scatter.2.cloned.1.call-start
  92.6 0.1 dynamic-slice_bitcast_fusion
  92.7 0.3 broadcast_compare_fusion
  93.0 0.7 eq.57
  93.8 32.2 %all-reduce.5.cloned.1.call-done = f32[1024,64]{0,1:T(8,128)} async-done(((f32[1024,64]{0,1:T(8,128)}), f32[1024,64]{0,1:T(8,128)}) %all-reduce.5.cloned.1.call-update) | async-done | bytes 262160 | tf_op jit(solution)/shard_map/psum | solution.py:82
  126.0 1.0 multiply_add_fusion
  126.9 3.6 %fusion.12 = f32[1024,768]{0,1:T(8,128)S(1)} fusion(f32[1024,64]{0,1:T(8,128)S(1)} %multiply_add_fusion, f32[2048,768]{0,1:T(8,128)} %copy-done.1), kind=kLoop, calls=%fused_computation.22 | loop fusion | flops 3932160 | bytes 9699328 | tf_op jit(solution)/shard_map/sub | solution.py:84
  130.6 0.5 fusion.19
  131.1 1.5 fusion.16
  132.7 25.1 %reduce-scatter.2.cloned.1.call-done = f32[256,224]{0,1:T(8,128)} async-done(((f32[1024,224]{0,1:T(8,128)}), f32[256,224]{0,1:T(8,128)}) %reduce-scatter.2.cloned.1.call-update) | async-done | bytes 229392 | tf_op jit(solution)/shard_map/reduce_scatter | solution.py:88
  157.8 1.8 copy.47
  159.6 9.6 %all-to-all-start.1 = ((f32[32,8,224]{2,1,0:T(8,128)}), f32[32,8,224]{2,1,0:T(8,128)S(1)}, u32[]{:S(2)}, u32[]{:S(2)}) async-start(f32[32,8,224]{2,1,0:T(8,128)} %bitcast.5), calls=%async_computation.2 | async-start | bytes 524288 | tf_op jit(solution)/shard_map/all_to_all | solution.py:91
  169.2 1.2 broadcast_and_fusion
  170.4 9.2 %all-to-all-done.1 = f32[32,8,224]{2,1,0:T(8,128)S(1)} async-done(((f32[32,8,224]{2,1,0:T(8,128)}), f32[32,8,224]{2,1,0:T(8,128)S(1)}, u32[]{:S(2)}, u32[]{:S(2)}) %all-to-all-start.1) | async-done | bytes 229408 | tf_op jit(solution)/shard_map/all_to_all | solution.py:91
  179.6 0.3 copy.48
  179.9 0.6 copy.49
  180.5 1.3 reshape.241
  181.8 0.2 pad_slice_fusion
  181.9 0.2 copy.50
  182.2 0.8 constant_dynamic-update-slice_fusion.4
  183.0 0.2 copy.51
  183.2 0.2 copy.52
  183.4 0.2 copy.53
  183.7 0.2 copy.54
  183.9 0.7 constant_dynamic-update-slice_fusion.3
  184.6 0.8 constant_dynamic-update-slice_fusion.2
  185.4 0.8 constant_dynamic-update-slice_fusion.1
  186.1 0.7 constant_dynamic-update-slice_fusion
  186.9 1.9 fusion.22
  188.8 2.4 %fusion.17 = f32[144,256]{1,0:T(8,128)S(1)} fusion(f32[144,256]{1,0:T(8,128)S(1)} %fusion.22, pred[2560,256]{1,0:T(8,128)(4,1)S(1)} %bitcast.60, f32[144,2560]{1,0:T(8,128)} %constant_dynamic-update-slice_fusion), kind=kOutput, calls=%fused_computation.31 | convolution fusion | flops 190291968 | bytes 2424832 | tf_op jit(solution)/shard_map/dot_general | solution.py:37
  191.2 5.7 %collective-permute-start = (f32[8,12,256]{2,1,0:T(8,128)S(1)}, f32[8,12,256]{2,1,0:T(8,128)S(1)}, u32[]{:S(2)}, u32[]{:S(2)}) collective-permute-start(f32[8,12,256]{2,1,0:T(8,128)S(1)} %get-tuple-element.12), channel_id=1, source_target_pairs={{128,0},{129,1},{130,2},{131,3},{132,4},{133,5},{134,6},{135,7},{1... | collective-permute-start | bytes 294920 | tf_op jit(solution)/shard_map/ppermute | solution.py:100
  196.9 0.7 fusion.60
  211.1 0.3 fusion.28
  211.3 0.7 fusion.36
  212.1 0.9 copy.55
  (31 shorter events, 0.5 us)
Async XLA Ops:
  6.5 86.1 %copy-start = (s32[16,8192]{1,0:T(8,128)S(1)}, s32[16,8192]{1,0:T(8,128)}, u32[]{:S(2)}) copy-start(s32[16,8192]{1,0:T(8,128)} %param.7) | copy-start | bytes 1572868
  15.4 5.4 %copy-start.5 = (s32[1024]{0:T(1024)S(1)}, s32[1024]{0:T(1024)}, u32[]{:S(2)}) copy-start(s32[1024]{0:T(1024)} %param.6) | copy-start | bytes 12292
  15.4 40.8 %all-to-all-start = ((bf16[2,256,12,256]{1,0,2,3:T(2,128)(2,1)}), bf16[2,256,12,256]{1,0,2,3:T(2,128)(2,1)}, u32[]{:S(2)}, u32[]{:S(2)}) async-start(bf16[2,256,12,256]{1,0,2,3:T(2,128)(2,1)} %copy.44), calls=%async_computation | async-start | bytes 6291456 | tf_op jit(solution)/shard_map/all_to_all | solution.py:72
  20.5 105.4 %all-reduce.5.cloned.1.call-start = ((), (), s32[]{:S(2)}) async-start(), calls=%async_computation.3 | async-start | bytes 524288 | tf_op jit(solution)/shard_map/psum | solution.py:82
  85.9 3.7 %copy-start.1 = (f32[2048,768]{0,1:T(8,128)}, f32[2048,768]{0,1:T(8,128)S(1)}, u32[]{:S(2)}) copy-start(f32[2048,768]{0,1:T(8,128)S(1)} %fusion) | copy-start | bytes 18874372
  92.4 65.4 %reduce-scatter.2.cloned.1.call-start = ((), (), s32[]{:S(2)}) async-start(), calls=%async_computation.4 | async-start | bytes 1146880 | tf_op jit(solution)/shard_map/reduce_scatter | solution.py:88
  131.1 1.5 copy-start.3
  159.6 20.0 %all-to-all-start.1 = ((f32[32,8,224]{2,1,0:T(8,128)}), f32[32,8,224]{2,1,0:T(8,128)S(1)}, u32[]{:S(2)}, u32[]{:S(2)}) async-start(f32[32,8,224]{2,1,0:T(8,128)} %bitcast.5), calls=%async_computation.2 | async-start | bytes 524288 | tf_op jit(solution)/shard_map/all_to_all | solution.py:91
  183.2 3.7 %copy-start.2 = (pred[5,32,16,256]{3,2,1,0:T(8,128)(4,1)S(1)}, pred[5,32,16,256]{3,2,1,0:T(8,128)(4,1)}, u32[]{:S(2)}) copy-start(pred[5,32,16,256]{3,2,1,0:T(8,128)(4,1)} %broadcast_and_fusion) | copy-start | bytes 1966084
  186.9 10.0 %copy-start.4 = (s32[3,2]{0,1:T(2,128)S(1)}, s32[3,2]{0,1:T(2,128)}, u32[]{:S(2)}) copy-start(s32[3,2]{0,1:T(2,128)} %param.9) | copy-start | bytes 76
  191.2 19.8 %collective-permute-start = (f32[8,12,256]{2,1,0:T(8,128)S(1)}, f32[8,12,256]{2,1,0:T(8,128)S(1)}, u32[]{:S(2)}, u32[]{:S(2)}) collective-permute-start(f32[8,12,256]{2,1,0:T(8,128)S(1)} %get-tuple-element.12), channel_id=1, source_target_pairs={{128,0},{129,1},{130,2},{131,3},{132,4},{133,5},{134,6},{135,7},{1... | collective-permute-start | bytes 294920 | tf_op jit(solution)/shard_map/ppermute | solution.py:100
Sparse Core Ops, SparseCore 0:
  92.5 33.3 all-reduce.4
  132.7 25.0 reduce-scatter.1
where the time goes:
time: 221 us; the launch traced here: 220 us
  waiting for transfers between devices  82.9 us (38%)
  local copies, waits for them, and re-layouts  34 us (15%)
  other arithmetic  32.1 us (15%)
  between operations  27.2 us (12%)
  matrix products  23.1 us (10%)
  starting transfers between devices  20.6 us (9%)
    psum x1, waiting for transfers between devices, per_device(): totals = lax.psum(jnp.sum(power, axis=1), 'section')  32.2 us
    reduce_scatter x1, waiting for transfers between devices, per_device(): summed = lax.psum_scatter(partial, 'feed', scatter_dimension=0, tiled=True)  25.1 us
    another operation x1, other arithmetic  19 us
    dot_general x1, matrix products, per_device(): product = jnp.dot(table, flat, preferred_element_type=jnp.float32)  16.8 us
    all_to_all x1, waiting for transfers between devices, per_device(): lax.all_to_all(voltages, 'feed', split_axis=3, concat_axis=1, tiled=True)  16.4 us
    unnamed x17, local copies, waits for them, and re-layouts  12.7 us
    all_to_all x1, starting transfers between devices, per_device(): lax.all_to_all(blocks, 'chan', split_axis=0, concat_axis=0, tiled=True)  9.56 us
    all_to_all x1, waiting for transfers between devices, per_device(): lax.all_to_all(blocks, 'chan', split_axis=0, concat_axis=0, tiled=True)  9.17 us
  transfers between devices with their start and end apart: 5, of which 4 were waited for; matrix products, arithmetic and copies ran while one was open for 10% of the time, Pallas kernels for 0%

commit v1 on v0

--- a/solution.py
+++ b/solution.py
@@ -79,7 +79,7 @@
     imag_part = product[NF:]
     power = (real_part * real_part + imag_part * imag_part).reshape(NF, span_t, local)
     section_count = lax.axis_size("section")
-    totals = lax.psum(jnp.sum(power, axis=1), "section")
+    totals = jnp.sum(lax.all_gather(jnp.sum(power, axis=1), "section"), axis=0)
     level = totals / (span_t * section_count)
     normed = power / (level[:, None, :] + EPSILON) - 1.0
     start = lax.axis_index("chan") * SUBCH + lax.axis_index("feed") * local

time: 221 us -> 192 us (0.87)
  waiting for transfers between devices: 82.9 us -> 49.6 us
  blocking collectives: 0 us -> 5.28 us
    psum x1 -> x0, waiting for transfers between devices: 32.2 us -> none  [per_device(): totals = lax.psum(jnp.sum(power, axis=1), 'section')]
    all_gather x0 -> x1, blocking collectives: none -> 5.28 us  [per_device(): totals = jnp.sum(lax.all_gather(jnp.sum(power, axis=1), 'section'), axis=0)]
  transfers between devices with their start and end apart: 5 -> 4, of which waited for: 4 -> 3; matrix products, arithmetic and copies ran while one was open for 10% -> 12% of each run, Pallas kernels for 0% -> 0%
where the time goes in v1:
time: 192 us; the launch traced here: 191 us
  waiting for transfers between devices  49.6 us (26%)
  local copies, waits for them, and re-layouts  34.5 us (18%)
  other arithmetic  31 us (16%)
  between operations  27.1 us (14%)
  matrix products  23.1 us (12%)
  starting transfers between devices  20.4 us (11%)
  blocking collectives  5.28 us (3%)
    reduce_scatter x1, waiting for transfers between devices, per_device(): summed = lax.psum_scatter(partial, 'feed', scatter_dimension=0, tiled=True)  25.2 us
    another operation x1, other arithmetic  19 us
    dot_general x1, matrix products, per_device(): product = jnp.dot(table, flat, preferred_element_type=jnp.float32)  16.8 us
    all_to_all x1, waiting for transfers between devices, per_device(): lax.all_to_all(voltages, 'feed', split_axis=3, concat_axis=1, tiled=True)  15.2 us
    unnamed x17, local copies, waits for them, and re-layouts  12.8 us
    all_to_all x1, starting transfers between devices, per_device(): lax.all_to_all(blocks, 'chan', split_axis=0, concat_axis=0, tiled=True)  9.57 us
    all_to_all x1, waiting for transfers between devices, per_device(): lax.all_to_all(blocks, 'chan', split_axis=0, concat_axis=0, tiled=True)  9.17 us
    all_to_all x2, local copies, waits for them, and re-layouts, per_device(): lax.all_to_all(voltages, 'feed', split_axis=3, concat_axis=1, tiled=True)  6.73 us
  transfers between devices with their start and end apart: 4, of which 3 were waited for; matrix products, arithmetic and copies ran while one was open for 12% of the time, Pallas kernels for 0%

profile of v1, /device:TPU:1, one launch (start us, length us, event | category | flops | bytes accessed | tf_op | source)
XLA Modules:
  0.0 190.9 jit_solution(1609677396335200799)
XLA Ops:
  6.5 8.9 %copy.44 = bf16[2,256,12,256]{1,0,2,3:T(2,128)(2,1)} copy(bf16[2,256,12,256]{3,1,2,0:T(8,128)(2,1)} %param.5) | data formatting | bytes 6291456 | tf_op args[0]
  15.4 5.1 %all-to-all-start = ((bf16[2,256,12,256]{1,0,2,3:T(2,128)(2,1)}), bf16[2,256,12,256]{1,0,2,3:T(2,128)(2,1)}, u32[]{:S(2)}, u32[]{:S(2)}) async-start(bf16[2,256,12,256]{1,0,2,3:T(2,128)(2,1)} %copy.44), calls=%async_computation | async-start | bytes 6291456 | tf_op jit(solution)/shard_map/all_to_all | solution.py:72
  20.6 0.1 iota_add_fusion
  20.7 0.1 add.156
  20.8 0.1 dynamic-slice_bitcast_fusion
  20.9 0.3 broadcast_compare_fusion
  21.3 0.7 eq.57
  22.0 19.0 %fusion.14 = (bf16[1024,1024]{1,0:T(8,128)(2,1)S(1)}, bf16[1024,1024]{1,0:T(8,128)(2,1)}, bf16[1024,1024]{1,0:T(8,128)(2,1)}) fusion(s32[1024]{0:T(1024)S(1)} %copy-done.5, s32[1024]{0:T(1024)S(1)} %add.156), kind=kLoop, calls=%fused_computation.25 | loop fusion | flops 18874368 | bytes 6299648 | tf_op jit(solution)/shard_map/convert.5
  41.0 15.2 %all-to-all-done = bf16[2,256,12,256]{1,0,2,3:T(2,128)(2,1)} async-done(((bf16[2,256,12,256]{1,0,2,3:T(2,128)(2,1)}), bf16[2,256,12,256]{1,0,2,3:T(2,128)(2,1)}, u32[]{:S(2)}, u32[]{:S(2)}) %all-to-all-start) | async-done | bytes 3145760 | tf_op jit(solution)/shard_map/all_to_all | solution.py:72
  56.2 2.6 %copy.45 = bf16[2,256,12,256]{1,3,2,0:T(8,128)(2,1)S(1)} copy(bf16[2,256,12,256]{1,0,2,3:T(2,128)(2,1)} %all-to-all-done) | data formatting | bytes 6291456 | tf_op jit(solution)/shard_map/all_to_all | solution.py:72
  58.9 4.1 %copy.46 = bf16[2,4,256,12,64]{2,1,0,4,3:T(4,128)(2,1)} copy(bf16[2,4,256,12,64]{2,4,1,3,0:T(8,128)(2,1)S(1)} %bitcast.58) | data formatting | bytes 6291456 | tf_op jit(solution)/shard_map/all_to_all | solution.py:72
  63.0 6.1 %reshape.240 = bf16[2048,768]{0,1:T(8,128)(2,1)} reshape(bf16[2,4,256,12,64]{2,1,0,4,3:T(4,128)(2,1)} %copy.46) | data formatting | bytes 6291456 | tf_op jit(solution)/shard_map/reshape | solution.py:76
  69.1 16.8 %fusion = f32[2048,768]{0,1:T(8,128)S(1)} fusion(bf16[2048,768]{0,1:T(8,128)(2,1)} %reshape.240, bf16[1024,1024]{1,0:T(8,128)(2,1)} %get-tuple-element.16, bf16[1024,1024]{1,0:T(8,128)(2,1)} %get-tuple-element.15, bf16[1024,1024]{1,0:T(8,128)(2,1)S(1)} %get-tuple-element.14), kind=kOutput, calls=%fused_computation | convolution fusion | flops 6476005376 | bytes 15728640 | tf_op jit(solution)/shard_map/dot_general | solution.py:77
  85.9 2.8 %fusion.11 = f32[1024,768]{0,1:T(8,128)} fusion(f32[2048,768]{0,1:T(8,128)S(1)} %fusion), kind=kLoop, calls=%fused_computation.19 | loop fusion | flops 2359296 | bytes 9437184 | tf_op jit(solution)/shard_map/add | solution.py:80
  88.8 0.8 copy-done.1
  89.6 2.1 %reduce_sum.18 = f32[1024,64]{0,1:T(8,128)S(1)} reduce(f32[1024,12,64]{0,2,1:T(8,128)} %bitcast.59, f32[]{:T(128)} %constant.80.clone.1), dimensions={1}, to_apply=%region_0.1 | reduce | flops 720896 | bytes 3407876 | tf_op jit(solution)/shard_map/reduce_sum | solution.py:82
  91.7 5.3 %all-gather = f32[2048,64]{0,1:T(8,128)S(1)} all-gather(f32[1024,64]{0,1:T(8,128)S(1)} %reduce_sum.18), channel_id=2, replica_groups=mesh['section'=2,'chan'=32,'feed'=4] {'section'}, dimensions={0}, use_global_device_ids=true | all-gather | bytes 786432 | tf_op jit(solution)/shard_map/all_gather | solution.py:82
  97.0 0.4 reshape.246
  97.4 0.6 reduce_sum.19
  98.1 3.6 %fusion.12 = f32[1024,768]{0,1:T(8,128)S(1)} fusion(f32[1024,64]{0,1:T(8,128)S(1)} %multiply_add_fusion, f32[2048,768]{0,1:T(8,128)} %copy-done.1), kind=kLoop, calls=%fused_computation.22 | loop fusion | flops 3932160 | bytes 9699328 | tf_op jit(solution)/shard_map/sub | solution.py:84
  101.8 0.5 fusion.19
  102.3 1.5 fusion.16
  103.9 25.2 %reduce-scatter.2.cloned.1.call-done = f32[256,224]{0,1:T(8,128)} async-done(((f32[1024,224]{0,1:T(8,128)}), f32[256,224]{0,1:T(8,128)}) %reduce-scatter.2.cloned.1.call-update) | async-done | bytes 229392 | tf_op jit(solution)/shard_map/reduce_scatter | solution.py:88
  129.1 1.8 copy.47
  130.8 9.6 %all-to-all-start.1 = ((f32[32,8,224]{2,1,0:T(8,128)}), f32[32,8,224]{2,1,0:T(8,128)S(1)}, u32[]{:S(2)}, u32[]{:S(2)}) async-start(f32[32,8,224]{2,1,0:T(8,128)} %bitcast.5), calls=%async_computation.2 | async-start | bytes 524288 | tf_op jit(solution)/shard_map/all_to_all | solution.py:91
  140.4 1.2 broadcast_and_fusion
  141.6 9.2 %all-to-all-done.1 = f32[32,8,224]{2,1,0:T(8,128)S(1)} async-done(((f32[32,8,224]{2,1,0:T(8,128)}), f32[32,8,224]{2,1,0:T(8,128)S(1)}, u32[]{:S(2)}, u32[]{:S(2)}) %all-to-all-start.1) | async-done | bytes 229408 | tf_op jit(solution)/shard_map/all_to_all | solution.py:91
  150.8 0.3 copy.48
  151.1 0.6 copy.49
  151.7 1.3 reshape.244
  153.0 0.2 pad_slice_fusion
  153.2 0.2 copy.50
  153.4 0.8 constant_dynamic-update-slice_fusion.4
  154.2 0.2 copy.51
  154.4 0.2 copy.52
  154.7 0.2 copy.53
  154.9 0.2 copy.54
  155.1 0.8 constant_dynamic-update-slice_fusion.3
  155.9 0.7 constant_dynamic-update-slice_fusion.2
  156.6 0.8 constant_dynamic-update-slice_fusion.1
  157.4 0.7 constant_dynamic-update-slice_fusion
  158.1 1.9 fusion.22
  160.0 2.3 %fusion.17 = f32[144,256]{1,0:T(8,128)S(1)} fusion(f32[144,256]{1,0:T(8,128)S(1)} %fusion.22, pred[2560,256]{1,0:T(8,128)(4,1)S(1)} %bitcast.62, f32[144,2560]{1,0:T(8,128)} %constant_dynamic-update-slice_fusion), kind=kOutput, calls=%fused_computation.31 | convolution fusion | flops 190291968 | bytes 2424832 | tf_op jit(solution)/shard_map/dot_general | solution.py:37
  162.4 5.7 %collective-permute-start = (f32[8,12,256]{2,1,0:T(8,128)S(1)}, f32[8,12,256]{2,1,0:T(8,128)S(1)}, u32[]{:S(2)}, u32[]{:S(2)}) collective-permute-start(f32[8,12,256]{2,1,0:T(8,128)S(1)} %get-tuple-element.12), channel_id=1, source_target_pairs={{128,0},{129,1},{130,2},{131,3},{132,4},{133,5},{134,6},{135,7},{1... | collective-permute-start | bytes 294920 | tf_op jit(solution)/shard_map/ppermute | solution.py:100
  168.1 0.7 fusion.60
  182.2 0.3 fusion.28
  182.5 0.7 fusion.36
  183.2 0.9 copy.55
  (31 shorter events, 0.5 us)
Async XLA Ops:
  6.5 14.3 %copy-start = (s32[16,8192]{1,0:T(8,128)S(1)}, s32[16,8192]{1,0:T(8,128)}, u32[]{:S(2)}) copy-start(s32[16,8192]{1,0:T(8,128)} %param.7) | copy-start | bytes 1572868
  15.4 6.6 %copy-start.5 = (s32[1024]{0:T(1024)S(1)}, s32[1024]{0:T(1024)}, u32[]{:S(2)}) copy-start(s32[1024]{0:T(1024)} %param.6) | copy-start | bytes 12292
  15.4 40.8 %all-to-all-start = ((bf16[2,256,12,256]{1,0,2,3:T(2,128)(2,1)}), bf16[2,256,12,256]{1,0,2,3:T(2,128)(2,1)}, u32[]{:S(2)}, u32[]{:S(2)}) async-start(bf16[2,256,12,256]{1,0,2,3:T(2,128)(2,1)} %copy.44), calls=%async_computation | async-start | bytes 6291456 | tf_op jit(solution)/shard_map/all_to_all | solution.py:72
  20.5 108.5 %reduce-scatter.2.cloned.1.call-start = ((), (), s32[]{:S(2)}) async-start(), calls=%async_computation.3 | async-start | bytes 1146880 | tf_op jit(solution)/shard_map/reduce_scatter | solution.py:88
  85.9 3.7 %copy-start.1 = (f32[2048,768]{0,1:T(8,128)}, f32[2048,768]{0,1:T(8,128)S(1)}, u32[]{:S(2)}) copy-start(f32[2048,768]{0,1:T(8,128)S(1)} %fusion) | copy-start | bytes 18874372
  102.3 1.5 copy-start.3
  130.8 20.0 %all-to-all-start.1 = ((f32[32,8,224]{2,1,0:T(8,128)}), f32[32,8,224]{2,1,0:T(8,128)S(1)}, u32[]{:S(2)}, u32[]{:S(2)}) async-start(f32[32,8,224]{2,1,0:T(8,128)} %bitcast.5), calls=%async_computation.2 | async-start | bytes 524288 | tf_op jit(solution)/shard_map/all_to_all | solution.py:91
  154.4 3.7 %copy-start.2 = (pred[5,32,16,256]{3,2,1,0:T(8,128)(4,1)S(1)}, pred[5,32,16,256]{3,2,1,0:T(8,128)(4,1)}, u32[]{:S(2)}) copy-start(pred[5,32,16,256]{3,2,1,0:T(8,128)(4,1)} %broadcast_and_fusion) | copy-start | bytes 1966084
  158.1 10.0 %copy-start.4 = (s32[3,2]{0,1:T(2,128)S(1)}, s32[3,2]{0,1:T(2,128)}, u32[]{:S(2)}) copy-start(s32[3,2]{0,1:T(2,128)} %param.9) | copy-start | bytes 76
  162.4 19.8 %collective-permute-start = (f32[8,12,256]{2,1,0:T(8,128)S(1)}, f32[8,12,256]{2,1,0:T(8,128)S(1)}, u32[]{:S(2)}, u32[]{:S(2)}) collective-permute-start(f32[8,12,256]{2,1,0:T(8,128)S(1)} %get-tuple-element.12), channel_id=1, source_target_pairs={{128,0},{129,1},{130,2},{131,3},{132,4},{133,5},{134,6},{135,7},{1... | collective-permute-start | bytes 294920 | tf_op jit(solution)/shard_map/ppermute | solution.py:100
Sparse Core Ops, SparseCore 0:
  103.9 25.0 reduce-scatter.1
